TPU v7x, 32 devices: a whole 2x2x4 slice. The times are simulated.
32 devices in a mesh: row: 4 (over x, core), col: 8 (over z, y).
Axes of the slice: x: 2, y: 2, z: 4, core: 2. Of those that a mesh axis runs over, the one named last changes fastest.
Arguments:
- matrix: float32 [24576, 24576], P('row', 'col'), may hold values from -6 to 6
Outputs:
- y_block: float32 [4, 24576], P(None, 'row')
- reflectors: float32 [4, 24576], P(None, 'row')
- t_factor: float32 [4, 4], replicated
All inputs are finite; a program needn't handle non-finite values.
Results may differ from a plain program's by a relative error of at most 0.0003.
Values sent between devices are 32-bit elements; how exact they have to be, the bound alone decides.
A program may use at most 128 MiB of HBM per device.

v0:
```python
import jax
import jax.numpy as jnp
from jax import lax
from jax.sharding import PartitionSpec as P

K = 4


precise = lax.Precision.HIGHEST


def from_root(value, axis, root):
    mine = lax.axis_index(axis) == root
    return lax.psum(jnp.where(mine, value, jnp.zeros_like(value)), axis)


def householder(pivot_value, squares):
    length = jnp.sqrt(pivot_value * pivot_value + squares)
    signed = jnp.where(pivot_value >= 0, 1.0, -1.0)
    diagonal = -signed * length
    factor = (diagonal - pivot_value) / diagonal
    return (factor, pivot_value - diagonal)


def finish(product, cross_dots, y_rows, t_block, factor, panel_step):
    new_column = factor * (product - jnp.dot(cross_dots, y_rows, precision=precise))
    t_column = -factor * jnp.dot(t_block, cross_dots, precision=precise)
    slots = jnp.arange(K, dtype=jnp.int32)
    t_column = jnp.where(slots == panel_step, factor, t_column)
    t_block = jnp.where(slots[None, :] == panel_step, t_column[:, None], t_block)
    y_rows = jnp.where(slots[:, None] == panel_step, new_column[None, :], y_rows)
    return (y_rows, t_block)


def multiply(matrix, whole_vector, col_start):
    cols_dev = matrix.shape[1]
    piece = lax.dynamic_slice_in_dim(whole_vector, col_start, cols_dev)
    partial_value = jnp.dot(matrix, piece, precision=precise)
    return lax.psum(partial_value, "col")


def on_device(matrix):
    rows_dev, cols_dev = matrix.shape
    row_index = lax.axis_index("row")
    row_start = row_index * rows_dev
    col_start = lax.axis_index("col") * cols_dev
    local_rows = row_start + jnp.arange(rows_dev, dtype=jnp.int32)
    slots = jnp.arange(K, dtype=jnp.int32)
    panel_rows = from_root(matrix[:, :K].T, "col", 0)

    def fetch(panel_step):
        return lax.dynamic_index_in_dim(panel_rows, panel_step, 0, keepdims=False)

    top_slots = jnp.arange(K + 1, dtype=jnp.int32)

    def advance(panel_step, carried):
        y_rows, v_rows, v_top, t_block = carried
        v_entry = lax.dynamic_index_in_dim(v_top, panel_step, 1, keepdims=False)
        column = fetch(panel_step) - jnp.dot(v_entry, y_rows, precision=precise)
        left_dots = lax.psum(jnp.dot(v_rows, column, precision=precise), "row")
        column = column - jnp.dot(
            jnp.dot(t_block.T, left_dots, precision=precise), v_rows, precision=precise
        )
        below = local_rows > panel_step + 1
        squares = jnp.sum(jnp.where(below, column * column, 0.0))
        top_rows = jnp.where(row_index == 0, column[: K + 1], 0.0)
        squares, top_rows = lax.psum((squares, top_rows), "row")
        pivot_value = lax.dynamic_index_in_dim(top_rows, panel_step + 1, 0, keepdims=False)
        factor, divisor = householder(pivot_value, squares)
        reflect = jnp.where(below, column / divisor, 0.0) + (local_rows == panel_step + 1).astype(
            jnp.float32
        )
        top_reflect = jnp.where(top_slots > panel_step + 1, top_rows / divisor, 0.0) + (
            top_slots == panel_step + 1
        ).astype(jnp.float32)
        whole_reflect = lax.all_gather(reflect, "row", axis=0, tiled=True)
        product = multiply(matrix, whole_reflect, col_start)
        cross_dots = lax.psum(jnp.dot(v_rows, reflect, precision=precise), "row")
        y_rows, t_block = finish(product, cross_dots, y_rows, t_block, factor, panel_step)
        v_rows = jnp.where(slots[:, None] == panel_step, reflect[None, :], v_rows)
        v_top = jnp.where(slots[:, None] == panel_step, top_reflect[None, :], v_top)
        return (y_rows, v_rows, v_top, t_block)

    start = (
        jnp.zeros((K, rows_dev), jnp.float32),
        jnp.zeros((K, rows_dev), jnp.float32),
        jnp.zeros((K, K + 1), jnp.float32),
        jnp.zeros((K, K), jnp.float32),
    )
    y_rows, v_rows, v_top, t_block = lax.fori_loop(0, K, advance, start)
    return (y_rows, v_rows, t_block)


def solution(mesh):
    return jax.shard_map(
        on_device,
        mesh=mesh,
        in_specs=(P("row", "col"),),
        out_specs=(P(None, "row"), P(None, "row"), P()),
        check_vma=False,
    )
```

profile of v0, /device:TPU:3, one launch (start us, length us, event | category | flops | bytes accessed | tf_op | source)
XLA Modules:
  0.0 608.5 jit_solution(6262619562696930310)
XLA Ops:
  7.2 2.1 slice.13
  9.3 1.2 copy.6
  10.5 0.7 select_bitcast_fusion
  11.2 70.2 %all-reduce.5.cloned.1.call-done = f32[4,6144]{1,0:T(4,128)} async-done(((f32[4,6144]{1,0:T(4,128)}), f32[4,6144]{1,0:T(4,128)}) %all-reduce.5.cloned.1.call-update) | async-done | bytes 98320 | tf_op jit(solution)/shard_map/psum | solution.py:14
  81.4 519.5 %while.23 = (s32[]{:T(128)}, f32[4,6144]{1,0:T(4,128)S(1)}, f32[4,6144]{1,0:T(4,128)S(1)}, f32[4,5]{0,1:T(8,128)S(1)}, f32[4,4]{1,0:T(4,128)S(1)}, /*index=5*/pr...) while((s32[]{:T(128)}, f32[4,6144]{1,0:T(4,128)S(1)}, ...), condition=%wide.region_8.9_spmd.clone.clone, body=%wide.region_1.8_spmd.clone.clone.sunk | while | flops 228293184 | bytes 77109064 | solution.py:90
  81.8 0.9 constant_dynamic-slice_fusion.2
  82.7 0.5 convolution_bitcast_fusion.7
  83.2 7.6 %psum.91 = f32[4]{0:T(128)S(1)} all-reduce(f32[4]{0:T(128)S(1)} %convolution_bitcast_fusion.7), channel_id=1, replica_groups=mesh['row'=4,'col'=8] {'row'}, use_global_device_ids=true, to_apply=%region_2.2 | all-reduce | flops 4 | bytes 32 | tf_op jit(solution)/shard_map/while/body/eval_jaxpr/psum | solution.py:60
  91.2 0.6 fusion.100
  91.8 6.5 %all-reduce.2 = (f32[5]{0:T(128)S(1)}, f32[]{:T(128)}) all-reduce(f32[5]{0:T(128)S(1)} %broadcast_select_fusion.7, f32[]{:T(128)} %get-tuple-element.465), channel_id=1, replica_groups=mesh['row'=4,'col'=8] {'row'}, use_global_device_ids=true, to_apply=%region_3.3 | all-reduce | flops 6 | bytes 48 | tf_op jit(solution)/shard_map/while/body/eval_jaxpr/psum | solution.py:67
  98.4 0.6 dynamic_slice.60
  102.5 0.5 convolution_bitcast_fusion.9
  103.0 5.8 psum.93
  109.0 5.8 all_gather.13
  114.8 65.6 %fusion.102 = f32[1,6144]{1,0:T(1,128)S(1)} fusion(f32[3072,1]{0,1:T(1,128)S(1)} %bitcast.93, f32[6144,3072]{1,0:T(8,128)} %get-tuple-element.510), kind=kOutput, calls=%fused_computation.66.clone.1 | convolution fusion | flops 226492416 | bytes 75534336 | tf_op jit(solution)/shard_map/while/body/eval_jaxpr/dot_general | solution.py:38
  180.4 28.0 %psum.92 = f32[6144]{0:T(1024)S(1)} all-reduce(f32[6144]{0:T(1024)S(1)} %bitcast.87), channel_id=1, replica_groups=mesh['row'=4,'col'=8] {'col'}, use_global_device_ids=true, to_apply=%region_6.6 | all-reduce | flops 6144 | bytes 49152 | tf_op jit(solution)/shard_map/while/body/eval_jaxpr/psum | solution.py:39
  209.2 0.9 constant_dynamic-slice_fusion.2
  210.2 0.5 convolution_bitcast_fusion.7
  210.7 12.4 %psum.91 = f32[4]{0:T(128)S(1)} all-reduce(f32[4]{0:T(128)S(1)} %convolution_bitcast_fusion.7), channel_id=1, replica_groups=mesh['row'=4,'col'=8] {'row'}, use_global_device_ids=true, to_apply=%region_2.2 | all-reduce | flops 4 | bytes 32 | tf_op jit(solution)/shard_map/while/body/eval_jaxpr/psum | solution.py:60
  223.5 0.6 fusion.100
  224.1 6.3 %all-reduce.2 = (f32[5]{0:T(128)S(1)}, f32[]{:T(128)}) all-reduce(f32[5]{0:T(128)S(1)} %broadcast_select_fusion.7, f32[]{:T(128)} %get-tuple-element.465), channel_id=1, replica_groups=mesh['row'=4,'col'=8] {'row'}, use_global_device_ids=true, to_apply=%region_3.3 | all-reduce | flops 6 | bytes 48 | tf_op jit(solution)/shard_map/while/body/eval_jaxpr/psum | solution.py:67
  230.4 0.6 dynamic_slice.60
  234.6 0.5 convolution_bitcast_fusion.9
  235.0 6.7 %psum.93 = f32[4]{0:T(128)S(1)} all-reduce(f32[4]{0:T(128)S(1)} %convolution_bitcast_fusion.9), channel_id=1, replica_groups=mesh['row'=4,'col'=8] {'row'}, use_global_device_ids=true, to_apply=%region_7.7 | all-reduce | flops 4 | bytes 32 | tf_op jit(solution)/shard_map/while/body/eval_jaxpr/psum | solution.py:78
  242.0 5.8 all_gather.13
  247.8 65.6 %fusion.102 = f32[1,6144]{1,0:T(1,128)S(1)} fusion(f32[3072,1]{0,1:T(1,128)S(1)} %bitcast.93, f32[6144,3072]{1,0:T(8,128)} %get-tuple-element.510), kind=kOutput, calls=%fused_computation.66.clone.1 | convolution fusion | flops 226492416 | bytes 75534336 | tf_op jit(solution)/shard_map/while/body/eval_jaxpr/dot_general | solution.py:38
  313.4 26.1 %psum.92 = f32[6144]{0:T(1024)S(1)} all-reduce(f32[6144]{0:T(1024)S(1)} %bitcast.87), channel_id=1, replica_groups=mesh['row'=4,'col'=8] {'col'}, use_global_device_ids=true, to_apply=%region_6.6 | all-reduce | flops 6144 | bytes 49152 | tf_op jit(solution)/shard_map/while/body/eval_jaxpr/psum | solution.py:39
  340.3 0.9 constant_dynamic-slice_fusion.2
  341.3 0.5 convolution_bitcast_fusion.7
  341.8 12.1 %psum.91 = f32[4]{0:T(128)S(1)} all-reduce(f32[4]{0:T(128)S(1)} %convolution_bitcast_fusion.7), channel_id=1, replica_groups=mesh['row'=4,'col'=8] {'row'}, use_global_device_ids=true, to_apply=%region_2.2 | all-reduce | flops 4 | bytes 32 | tf_op jit(solution)/shard_map/while/body/eval_jaxpr/psum | solution.py:60
  354.4 0.6 fusion.100
  355.0 6.3 %all-reduce.2 = (f32[5]{0:T(128)S(1)}, f32[]{:T(128)}) all-reduce(f32[5]{0:T(128)S(1)} %broadcast_select_fusion.7, f32[]{:T(128)} %get-tuple-element.465), channel_id=1, replica_groups=mesh['row'=4,'col'=8] {'row'}, use_global_device_ids=true, to_apply=%region_3.3 | all-reduce | flops 6 | bytes 48 | tf_op jit(solution)/shard_map/while/body/eval_jaxpr/psum | solution.py:67
  361.3 0.6 dynamic_slice.60
  365.4 0.5 convolution_bitcast_fusion.9
  365.9 6.0 psum.93
  372.1 5.8 all_gather.13
  377.9 65.6 %fusion.102 = f32[1,6144]{1,0:T(1,128)S(1)} fusion(f32[3072,1]{0,1:T(1,128)S(1)} %bitcast.93, f32[6144,3072]{1,0:T(8,128)} %get-tuple-element.510), kind=kOutput, calls=%fused_computation.66.clone.1 | convolution fusion | flops 226492416 | bytes 75534336 | tf_op jit(solution)/shard_map/while/body/eval_jaxpr/dot_general | solution.py:38
  443.5 26.1 %psum.92 = f32[6144]{0:T(1024)S(1)} all-reduce(f32[6144]{0:T(1024)S(1)} %bitcast.87), channel_id=1, replica_groups=mesh['row'=4,'col'=8] {'col'}, use_global_device_ids=true, to_apply=%region_6.6 | all-reduce | flops 6144 | bytes 49152 | tf_op jit(solution)/shard_map/while/body/eval_jaxpr/psum | solution.py:39
  470.4 0.9 constant_dynamic-slice_fusion.2
  471.9 12.1 %psum.91 = f32[4]{0:T(128)S(1)} all-reduce(f32[4]{0:T(128)S(1)} %convolution_bitcast_fusion.7), channel_id=1, replica_groups=mesh['row'=4,'col'=8] {'row'}, use_global_device_ids=true, to_apply=%region_2.2 | all-reduce | flops 4 | bytes 32 | tf_op jit(solution)/shard_map/while/body/eval_jaxpr/psum | solution.py:60
  484.5 0.6 fusion.100
  485.1 6.3 %all-reduce.2 = (f32[5]{0:T(128)S(1)}, f32[]{:T(128)}) all-reduce(f32[5]{0:T(128)S(1)} %broadcast_select_fusion.7, f32[]{:T(128)} %get-tuple-element.465), channel_id=1, replica_groups=mesh['row'=4,'col'=8] {'row'}, use_global_device_ids=true, to_apply=%region_3.3 | all-reduce | flops 6 | bytes 48 | tf_op jit(solution)/shard_map/while/body/eval_jaxpr/psum | solution.py:67
  491.4 0.6 dynamic_slice.60
  496.0 6.7 %psum.93 = f32[4]{0:T(128)S(1)} all-reduce(f32[4]{0:T(128)S(1)} %convolution_bitcast_fusion.9), channel_id=1, replica_groups=mesh['row'=4,'col'=8] {'row'}, use_global_device_ids=true, to_apply=%region_7.7 | all-reduce | flops 4 | bytes 32 | tf_op jit(solution)/shard_map/while/body/eval_jaxpr/psum | solution.py:78
  502.9 5.8 all_gather.13
  508.7 65.6 %fusion.102 = f32[1,6144]{1,0:T(1,128)S(1)} fusion(f32[3072,1]{0,1:T(1,128)S(1)} %bitcast.93, f32[6144,3072]{1,0:T(8,128)} %get-tuple-element.510), kind=kOutput, calls=%fused_computation.66.clone.1 | convolution fusion | flops 226492416 | bytes 75534336 | tf_op jit(solution)/shard_map/while/body/eval_jaxpr/dot_general | solution.py:38
  574.3 26.1 %psum.92 = f32[6144]{0:T(1024)S(1)} all-reduce(f32[6144]{0:T(1024)S(1)} %bitcast.87), channel_id=1, replica_groups=mesh['row'=4,'col'=8] {'col'}, use_global_device_ids=true, to_apply=%region_6.6 | all-reduce | flops 6144 | bytes 49152 | tf_op jit(solution)/shard_map/while/body/eval_jaxpr/psum | solution.py:39
  601.0 0.6 copy-done
  (77 shorter events, 7.2 us)
Async XLA Ops:
  7.2 74.3 %all-reduce.5.cloned.1.call-start = ((), (), s32[]{:S(2)}) async-start(), calls=%async_computation | async-start | bytes 196608 | tf_op jit(solution)/shard_map/psum | solution.py:14
  600.9 0.6 copy-start
  601.0 0.7 copy-start.1
  601.0 0.7 copy-start.2
Sparse Core Ops, SparseCore 0:
  11.9 69.4 all-reduce.4
where the time goes:
time: 617 us; the launch traced here: 608 us
  matrix products  271 us (44%)
  blocking collectives  224 us (36%)
  waiting for transfers between devices  70.2 us (11%)
  loops' own time  14.5 us (2%)
  between operations  14.1 us (2%)
  local copies, waits for them, and re-layouts  9.95 us (2%)
    dot_general x4, matrix products, multiply(): partial_value = jnp.dot(matrix, piece, precision=precise)  262 us
    psum x4, blocking collectives, multiply(): return lax.psum(partial_value, 'col')  106 us
    psum x1, waiting for transfers between devices, from_root(): return lax.psum(jnp.where(mine, value, jnp.zeros_like(value)), axis)  70.2 us
    psum x4, blocking collectives, advance(): left_dots = lax.psum(jnp.dot(v_rows, column, precision=precise), 'row')  44.3 us
    psum x4, blocking collectives, advance(): squares, top_rows = lax.psum((squares, top_rows), 'row')  25.4 us
    psum x4, blocking collectives, advance(): cross_dots = lax.psum(jnp.dot(v_rows, reflect, precision=precise), 'row')  25.2 us
    all_gather x4, blocking collectives, advance(): whole_reflect = lax.all_gather(reflect, 'row', axis=0, tiled=True)  23.2 us
    another operation x1, loops' own time, on_device(): y_rows, v_rows, v_top, t_block = lax.fori_loop(0, K, advance, start)  14.5 us
  transfers between devices with their start and end apart: 1, of which 1 were waited for; matrix products, arithmetic and copies ran while one was open for 0% of the time, Pallas kernels for 0%

commit v1 on v0

v1 whole, which is shorter than its diff:
```python
import functools

import jax
import jax.numpy as jnp
from jax import lax
from jax.experimental import pallas as pl
from jax.experimental.pallas import tpu as pltpu
from jax.sharding import PartitionSpec as P

K = 4
LANES = 128
MESH = pl.DeviceIdType.MESH
VMEM_BYTES = 67043328
SPARE_BYTES = 5 * 2**19


def plan(R, C, rows, cols):
    q = C // R
    m = cols // LANES
    G = 8 if m % 8 == 0 else m
    ng = m // G
    groups = q * ng
    ring = max(4, q)
    room = (VMEM_BYTES - SPARE_BYTES) // (LANES * cols * 4)
    sp = 0
    while (G - sp) * groups + ring > room:
        sp += 1
    return q, m, G, ng, groups, ring, sp


def lane_total(row):
    return jnp.sum(row, axis=-1, keepdims=True)


def kernel(
    R, C, a_hbm, y_ref, v_ref, t_ref,
    res, ring, acc, pan, av, xs, pbuf, rbuf, sbuf, rnd, vy, ob, vs, ys, ps,
    res_sem, ring_sem, pan_sem, pan_send, av_sem, p_send, p_recv, s_send, s_recv, o_send, o_recv,
):
    rows, cols = a_hbm.shape
    q, m, G, ng, groups, nring, sp = plan(R, C, rows, cols)
    rp = G - sp
    r = lax.axis_index("row")
    c = lax.axis_index("col")

    def send(src, dst, send_sem, recv_sem, tr, tc):
        same = jnp.logical_and(tr == r, tc == c)

        @pl.when(jnp.logical_not(same))
        def _():
            pltpu.make_async_remote_copy(
                src, dst, send_sem, recv_sem, device_id=(tr, tc), device_id_type=MESH
            ).start()

        @pl.when(same)
        def _():
            pltpu.make_async_copy(src, dst, recv_sem).start()

    def sent(src, dst, send_sem, recv_sem, tr, tc):
        same = jnp.logical_and(tr == r, tc == c)

        @pl.when(jnp.logical_not(same))
        def _():
            pltpu.make_async_remote_copy(
                src, dst, send_sem, recv_sem, device_id=(tr, tc), device_id_type=MESH
            ).wait_send()

    def arrived(ref, sem):
        pltpu.make_async_copy(ref, ref, sem).wait()

    def panel_copy(t):
        return pltpu.make_async_copy(
            a_hbm.at[pl.ds(pl.multiple_of(t * LANES, LANES), LANES), pl.ds(0, LANES)],
            ring.at[lax.div(t, m), :, pl.ds(pl.multiple_of(lax.rem(t, m) * LANES, LANES), LANES)],
            pan_sem,
        )

    @pl.when(c == 0)
    def _():
        @pl.loop(0, q * m)
        def _(t):
            panel_copy(t).start()

    def res_copy(g, i):
        row = pl.multiple_of((g * G + i) * LANES, LANES)
        k = g * rp + i
        return pltpu.make_async_copy(a_hbm.at[pl.ds(row, LANES)], res.at[k], res_sem.at[k])

    def ring_copy(seq):
        n = lax.rem(seq, groups * sp)
        g, u = lax.div(n, sp), lax.rem(n, sp)
        row = pl.multiple_of((g * G + rp + u) * LANES, LANES)
        slot = lax.rem(seq, nring)
        return pltpu.make_async_copy(a_hbm.at[pl.ds(row, LANES)], ring.at[slot], ring_sem.at[slot])

    @pl.loop(0, groups)
    def _(g):
        @pl.loop(0, rp)
        def _(i):
            res_copy(g, i).start()

    barrier = pltpu.get_barrier_semaphore()
    me = r * C + c

    @pl.loop(1, R * C)
    def _(k):
        t = lax.rem(me + k, R * C)
        pl.semaphore_signal(
            barrier, inc=1, device_id=(lax.div(t, C), lax.rem(t, C)), device_id_type=MESH
        )

    pl.semaphore_wait(barrier, R * C - 1)

    def panel_sends(act):
        for part in range(2):
            for piece in range(q):
                for tr in range(R):
                    first, count = (0, 1) if part == 0 else (1, K)
                    act(
                        pan.at[pl.ds(first, count), pl.ds(piece * ng, ng)],
                        av.at[pl.ds(first, count)],
                        pan_send.at[part, piece, tr],
                        av_sem.at[part],
                        jnp.int32(tr),
                        r * q + piece,
                    )

    @pl.when(c == 0)
    def _():
        arrived(ring.at[pl.ds(0, q)], pan_sem)

        @pl.loop(0, groups)
        def _(g):
            slot = lax.div(g, ng)
            for s in range(G):
                at = pl.multiple_of((lax.rem(g, ng) * G + s) * LANES, LANES)
                turned = ring[slot, :, pl.ds(at, LANES)].T
                for k in range(K + 1):
                    pan[k, g, s : s + 1, :] = turned[k : k + 1, :]

        panel_sends(send)

    if sp:
        for seq in range(min(nring, K * groups * sp)):
            ring_copy(jnp.int32(seq)).start()

    sub = lax.broadcasted_iota(jnp.int32, (G, LANES), 0)
    lane = lax.broadcasted_iota(jnp.int32, (G, LANES), 1)
    where_at = [c * cols + (n * G + sub) * LANES + lane for n in range(ng)]
    lane1 = lax.broadcasted_iota(jnp.int32, (1, LANES), 1)
    first_col = (jnp.zeros((1, LANES), jnp.int32) + c) == 0

    def load(ref, *at):
        return [ref[(*at, n)] for n in range(ng)]

    def store(ref, value, *at):
        for n in range(ng):
            ref[(*at, n)] = value[n]

    def pick(row, k):
        return lane_total(jnp.where(lane1 == k, row, 0.0))

    def dots(one, two):
        total = one[0] * two[0]
        for n in range(1, ng):
            total = total + one[n] * two[n]
        return jnp.sum(total, axis=0, keepdims=True)

    def less(value, scale, other):
        return [a - scale * b for a, b in zip(value, other)]

    def round_copy(j, k, o):
        tc = lax.rem(c + o, C)
        return pltpu.make_async_remote_copy(
            sbuf.at[j, k], rnd.at[j, k, c], s_send.at[j, k], s_recv.at[j, k],
            device_id=(r, tc), device_id_type=MESH,
        )

    def round_send(j, k):
        rnd[j, k, c] = sbuf[j, k]

        @pl.loop(1, C)
        def _(o):
            round_copy(j, k, o).start()

    def round_get(j, k):
        arrived(rnd.at[j, k, pl.ds(0, C - 1)], s_recv.at[j, k])
        total = rnd[j, k, 0]
        for n in range(1, C):
            total = total + rnd[j, k, n]
        return total

    def p_targets(j, g, act):
        piece, part = lax.div(g, ng), lax.rem(g, ng)
        for tr in range(R):
            act(
                pbuf.at[j, g], rbuf.at[j, c, part], p_send.at[j, g, tr], p_recv.at[j],
                jnp.int32(tr), r * q + piece,
            )

    def o_targets(j, act):
        for u in range(q):
            act(
                vy.at[j], ob.at[j, lax.rem(c, q)], o_send.at[j, u], o_recv.at[j],
                lax.div(c, q), r + R * u,
            )

    diag_sub = lax.broadcasted_iota(jnp.int32, (LANES, LANES), 0)
    diag_lane = lax.broadcasted_iota(jnp.int32, (LANES, LANES), 1)

    def times(chunk, s):
        total = None
        for t in range(m):
            term = chunk[:, t * LANES : (t + 1) * LANES] * xs[t // G, t % G : t % G + 1, :]
            total = term if total is None else total + term
        acc[s] = total

    def multiply_groups(j, low, high):
        @pl.loop(low, high)
        def _(g):
            cuts = [rp * u // max(sp, 1) for u in range(max(sp, 1) + 1)]
            for u in range(max(sp, 1)):
                @pl.loop(cuts[u], cuts[u + 1])
                def _(i):
                    if j == 0:
                        res_copy(g, i).wait()
                    times(res.at[g * rp + i], i)

                if sp:
                    seq = j * groups * sp + g * sp + u
                    ring_copy(seq).wait()
                    times(ring.at[lax.rem(seq, nring)], rp + u)

                    @pl.when(seq + nring < K * groups * sp)
                    def _():
                        ring_copy(seq + nring).start()

            for s in range(G):
                line = jnp.sum(acc[s], axis=1, keepdims=True)
                line = jnp.where(diag_sub == diag_lane, line, 0.0)
                pbuf[j, g, s : s + 1, :] = jnp.sum(line, axis=0, keepdims=True)
            p_targets(j, g, send)

    zero = jnp.zeros((1, 1), jnp.float32)
    v_top, t_cols = [], []
    arrived(av.at[pl.ds(0, 1)], av_sem.at[0])

    for j in range(K):
        x = load(av, j)
        for i in range(j):
            x = less(x, pick(v_top[i], j), load(ys, i))
        store(xs, [jnp.where(w > j + 1, a, 0.0) for w, a in zip(where_at, x)])
        x_top_row = jnp.where(first_col, x[0][0:1, :], 0.0)
        sbuf[j, 0] = jnp.zeros((8, LANES), jnp.float32)
        sbuf[j, 1] = jnp.zeros((8, LANES), jnp.float32)
        sbuf[j, 0 if j else 1, K + 1 : K + 2, :] = x_top_row

        if j:
            for i in range(j):
                sbuf[j, 0, i : i + 1, :] = dots(load(vs, i), x)
            round_send(j, 0)
            multiply_groups(j, 0, groups - 1)
            got = round_get(j, 0)
            left = [lane_total(got[i : i + 1, :]) for i in range(j)]
            w = []
            for k in range(j):
                total = zero
                for i in range(k + 1):
                    total = total + t_cols[k][i] * left[i]
                w.append(total)
            b, b_top = x, got[K + 1 : K + 2, :]
            for i in range(j):
                b = less(b, w[i], load(vs, i))
                b_top = b_top - w[i] * v_top[i]
        else:
            b, w = x, []
        b = [jnp.where(at > j + 1, a, 0.0) for at, a in zip(where_at, b)]
        for i in range(j):
            sbuf[j, 1, i : i + 1, :] = dots(load(vs, i), b)
        sbuf[j, 1, K : K + 1, :] = dots(b, b)
        round_send(j, 1)
        multiply_groups(j, groups - 1 if j else 0, groups)

        got = round_get(j, 1)
        if j == 0:
            b_top = got[K + 1 : K + 2, :]
            arrived(av.at[pl.ds(1, K)], av_sem.at[1])
        squares = lane_total(got[K : K + 1, :])
        pivot = pick(b_top, j + 1)
        length = jnp.sqrt(pivot * pivot + squares)
        beta = -jnp.where(pivot >= 0, 1.0, -1.0) * length
        tau = (beta - pivot) / beta
        div = pivot - beta
        cross = [lane_total(got[i : i + 1, :]) / div + pick(v_top[i], j + 1) for i in range(j)]
        v = [a / div + jnp.where(at == j + 1, 1.0, 0.0) for at, a in zip(where_at, b)]
        store(vs, v, j)
        store(vy, v, j, 1)
        new_top = jnp.where(lane1 > j + 1, b_top / div, 0.0) + jnp.where(lane1 == j + 1, 1.0, 0.0)

        arrived(rbuf.at[j], p_recv.at[j])
        p = load(rbuf, j, 0)
        for n in range(1, C):
            p = [a + b_ for a, b_ in zip(p, load(rbuf, j, n))]
        for i in range(j):
            p = less(p, w[i], load(ps, i))
        for k in range(j + 2):
            if j:
                back = zero
                for i in range(j):
                    back = back - w[i] * pick(v_top[i], k)
                p = less(p, back, load(av, k))
        p = [a / div + e for a, e in zip(p, load(av, j + 1))]
        store(ps, p, j)
        y = p
        for i in range(j):
            y = less(y, cross[i], load(ys, i))
        y = [tau * a for a in y]
        store(ys, y, j)
        store(vy, y, j, 0)
        o_targets(j, send)
        column = []
        for i in range(j):
            total = zero
            for k in range(i, j):
                total = total + t_cols[k][i] * cross[k]
            column.append(-tau * total)
        t_cols.append(column + [tau])
        v_top.append(new_top)

    ti = lax.broadcasted_iota(jnp.int32, (K, K), 0)
    tj = lax.broadcasted_iota(jnp.int32, (K, K), 1)
    t_all = jnp.zeros((K, K), jnp.float32)
    for j in range(K):
        for i in range(j + 1):
            t_all = jnp.where(jnp.logical_and(ti == i, tj == j), t_cols[j][i], t_all)
    t_ref[...] = t_all

    for j in range(K):
        arrived(ob.at[j], o_recv.at[j])
    for h in range(q):
        for n in range(ng):
            for s in range(G):
                at = ((h * ng + n) * G + s) * LANES
                for j in range(K):
                    y_ref[j : j + 1, at : at + LANES] = ob[j, h, 0, n, s : s + 1, :]
                    v_ref[j : j + 1, at : at + LANES] = ob[j, h, 1, n, s : s + 1, :]

    @pl.when(c == 0)
    def _():
        panel_sends(sent)

    for j in range(K):
        for k in range(0 if j else 1, 2):
            arrived(rnd.at[j, k, pl.ds(0, C - 1)], s_send.at[j, k])

        @pl.loop(0, groups)
        def _(g):
            p_targets(j, g, sent)

        o_targets(j, sent)


def solution(mesh):
    R, C = mesh.shape["row"], mesh.shape["col"]

    def on_device(matrix):
        rows, cols = matrix.shape
        q, m, G, ng, groups, ring, sp = plan(R, C, rows, cols)
        f32 = lambda *shape: pltpu.VMEM(shape, jnp.float32)
        dma = lambda *shape: pltpu.SemaphoreType.DMA(shape)
        nres = groups * (G - sp)
        return pl.pallas_call(
            functools.partial(kernel, R, C),
            out_shape=(
                jax.ShapeDtypeStruct((K, rows), jnp.float32),
                jax.ShapeDtypeStruct((K, rows), jnp.float32),
                jax.ShapeDtypeStruct((K, K), jnp.float32),
            ),
            in_specs=[pl.BlockSpec(memory_space=pl.ANY)],
            out_specs=(pl.BlockSpec(memory_space=pltpu.VMEM),) * 3,
            scratch_shapes=[
                f32(nres, LANES, cols),
                f32(ring, LANES, cols),
                f32(G, LANES, LANES),
                f32(K + 1, groups, G, LANES),
                f32(K + 1, ng, G, LANES),
                f32(ng, G, LANES),
                f32(K, groups, G, LANES),
                f32(K, C, ng, G, LANES),
                f32(K, 2, 8, LANES),
                f32(K, 2, C, 8, LANES),
                f32(K, 2, ng, G, LANES),
                f32(K, q, 2, ng, G, LANES),
                f32(K, ng, G, LANES),
                f32(K, ng, G, LANES),
                f32(K, ng, G, LANES),
                dma(nres),
                dma(ring),
                pltpu.SemaphoreType.DMA,
                dma(2, q, R),
                dma(2),
                dma(K, groups, R),
                dma(K),
                dma(K, 2),
                dma(K, 2),
                dma(K, q),
                dma(K),
            ],
            compiler_params=pltpu.CompilerParams(
                collective_id=0, has_side_effects=True, vmem_limit_bytes=VMEM_BYTES
            ),
        )(matrix)

    return jax.shard_map(
        on_device,
        mesh=mesh,
        in_specs=(P("row", "col"),),
        out_specs=(P(None, "row"), P(None, "row"), P()),
        check_vma=False,
    )
```

time: 617 us -> 76.5 us (0.12); the launches traced: 608 us -> 76.3 us
  matrix products: 271 us -> 0 us
  blocking collectives: 224 us -> 0 us
  Pallas kernels: 0 us -> 71.4 us
  waiting for transfers between devices: 70.2 us -> 0 us
  loops' own time: 14.5 us -> 0 us
  between operations: 14.1 us -> 0.64 us
    dot_general x32 -> x0, matrix products: 271 us -> none  [the longest x4 262 us: multiply(): partial_value = jnp.dot(matrix, piece, precision=precise)]
    psum x16 -> x0, blocking collectives: 201 us -> none  [the longest x4 106 us: multiply(): return lax.psum(partial_value, 'col')]
    pallas_call x0 -> x1, Pallas kernels: none -> 71.4 us  [on_device(): pl.pallas_call(functools.partial(kernel, R, C), out_shape=(jax.ShapeDtype...]
    psum x1 -> x0, waiting for transfers between devices: 70.2 us -> none  [from_root(): return lax.psum(jnp.where(mine, value, jnp.zeros_like(value)), axis)]
    all_gather x4 -> x0, blocking collectives: 23.2 us -> none  [advance(): whole_reflect = lax.all_gather(reflect, 'row', axis=0, tiled=True)]
    another operation x1 -> x0, loops' own time: 14.5 us -> none  [on_device(): y_rows, v_rows, v_top, t_block = lax.fori_loop(0, K, advance, start)]
  transfers between devices with their start and end apart: 1 -> 0, of which waited for: 1 -> 0; matrix products, arithmetic and copies ran while one was open for 0% -> 0% of each run, Pallas kernels for 0% -> 0%
where the time goes in v1:
time: 76.5 us; the launch traced here: 76.3 us
  Pallas kernels  71.4 us (93%)
  local copies, waits for them, and re-layouts  4.31 us (6%)
    pallas_call x1, Pallas kernels, on_device(): pl.pallas_call(functools.partial(kernel, R, C), out_shape=(jax.ShapeDtype...  71.4 us
    unnamed x3, local copies, waits for them, and re-layouts  4.31 us

profile of v1, /device:TPU:3, one launch (start us, length us, event | category | flops | bytes accessed | tf_op | source)
XLA Modules:
  0.0 76.3 jit_solution(16181589576683753566)
XLA Ops:
  0.6 71.4 %shard_map.38 = (f32[4,6144]{1,0:T(4,128)}, f32[4,6144]{1,0:T(4,128)}, f32[4,4]{1,0:T(4,128)}) custom-call(f32[6144,3072]{1,0:T(8,128)} %a_hbm.1), custom_call_target="tpu_custom_call" | custom-call | tf_op jit(solution)/shard_map/pallas_call | solution.py:372
  72.0 1.5 %copy.7 = f32[4,6144]{1,0:T(4,128)} copy(f32[4,6144]{1,0:T(4,128)} %get-tuple-element.6) | data formatting | bytes 196608
  73.6 1.5 %copy.8 = f32[4,6144]{1,0:T(4,128)} copy(f32[4,6144]{1,0:T(4,128)} %get-tuple-element.7) | data formatting | bytes 196608
  75.1 1.2 %copy.9 = f32[4,4]{1,0:T(4,128)} copy(f32[4,4]{1,0:T(4,128)} %get-tuple-element.8) | data formatting | bytes 128

commit v2 on v1

--- a/solution.py
+++ b/solution.py
@@ -33,7 +33,7 @@
 
 
 def kernel(
-    R, C, a_hbm, y_ref, v_ref, t_ref,
+    R, C, a_hbm, o_ref, t_ref,
     res, ring, acc, pan, av, xs, pbuf, rbuf, sbuf, rnd, vy, ob, vs, ys, ps,
     res_sem, ring_sem, pan_sem, pan_send, av_sem, p_send, p_recv, s_send, s_recv, o_send, o_recv,
 ):
@@ -108,8 +108,6 @@
         pl.semaphore_signal(
             barrier, inc=1, device_id=(lax.div(t, C), lax.rem(t, C)), device_id_type=MESH
         )
-
-    pl.semaphore_wait(barrier, R * C - 1)
 
     def panel_sends(act):
         for part in range(2):
@@ -138,6 +136,10 @@
                 for k in range(K + 1):
                     pan[k, g, s : s + 1, :] = turned[k : k + 1, :]
 
+    pl.semaphore_wait(barrier, R * C - 1)
+
+    @pl.when(c == 0)
+    def _():
         panel_sends(send)
 
     if sp:
@@ -242,13 +244,13 @@
             p_targets(j, g, send)
 
     zero = jnp.zeros((1, 1), jnp.float32)
+    early = groups - max(1, groups // 3)
     v_top, t_cols = [], []
     arrived(av.at[pl.ds(0, 1)], av_sem.at[0])
 
     for j in range(K):
-        x = load(av, j)
-        for i in range(j):
-            x = less(x, pick(v_top[i], j), load(ys, i))
+        if j == 0:
+            x = load(av, 0)
         store(xs, [jnp.where(w > j + 1, a, 0.0) for w, a in zip(where_at, x)])
         x_top_row = jnp.where(first_col, x[0][0:1, :], 0.0)
         sbuf[j, 0] = jnp.zeros((8, LANES), jnp.float32)
@@ -259,7 +261,8 @@
             for i in range(j):
                 sbuf[j, 0, i : i + 1, :] = dots(load(vs, i), x)
             round_send(j, 0)
-            multiply_groups(j, 0, groups - 1)
+            o_targets(j - 1, send)
+            multiply_groups(j, 0, early)
             got = round_get(j, 0)
             left = [lane_total(got[i : i + 1, :]) for i in range(j)]
             w = []
@@ -279,7 +282,7 @@
             sbuf[j, 1, i : i + 1, :] = dots(load(vs, i), b)
         sbuf[j, 1, K : K + 1, :] = dots(b, b)
         round_send(j, 1)
-        multiply_groups(j, groups - 1 if j else 0, groups)
+        multiply_groups(j, early if j else 0, groups)
 
         got = round_get(j, 1)
         if j == 0:
@@ -297,27 +300,7 @@
         store(vy, v, j, 1)
         new_top = jnp.where(lane1 > j + 1, b_top / div, 0.0) + jnp.where(lane1 == j + 1, 1.0, 0.0)
 
-        arrived(rbuf.at[j], p_recv.at[j])
-        p = load(rbuf, j, 0)
-        for n in range(1, C):
-            p = [a + b_ for a, b_ in zip(p, load(rbuf, j, n))]
-        for i in range(j):
-            p = less(p, w[i], load(ps, i))
-        for k in range(j + 2):
-            if j:
-                back = zero
-                for i in range(j):
-                    back = back - w[i] * pick(v_top[i], k)
-                p = less(p, back, load(av, k))
-        p = [a / div + e for a, e in zip(p, load(av, j + 1))]
-        store(ps, p, j)
-        y = p
-        for i in range(j):
-            y = less(y, cross[i], load(ys, i))
-        y = [tau * a for a in y]
-        store(ys, y, j)
-        store(vy, y, j, 0)
-        o_targets(j, send)
+        v_top.append(new_top)
         column = []
         for i in range(j):
             total = zero
@@ -325,7 +308,37 @@
                 total = total + t_cols[k][i] * cross[k]
             column.append(-tau * total)
         t_cols.append(column + [tau])
-        v_top.append(new_top)
+
+        fix = [jnp.zeros((G, LANES), jnp.float32)] * ng
+        for i in range(j):
+            fix = less(fix, w[i], load(ps, i))
+        for k in range(j + 2 if j else 0):
+            back = zero
+            for i in range(j):
+                back = back - w[i] * pick(v_top[i], k)
+            fix = less(fix, back, load(av, k))
+        y_fix = load(av, j + 1)
+        for i in range(j):
+            y_fix = less(y_fix, cross[i], load(ys, i))
+        if j + 1 < K:
+            x = load(av, j + 1)
+            for i in range(j):
+                x = less(x, pick(v_top[i], j + 1), load(ys, i))
+            entry = pick(new_top, j + 1)
+
+        arrived(rbuf.at[j], p_recv.at[j])
+        p = load(rbuf, j, 0)
+        for n in range(1, C):
+            p = [a + b_ for a, b_ in zip(p, load(rbuf, j, n))]
+        p = [(a + e) / div for a, e in zip(p, fix)]
+        y = [tau * (a + e) for a, e in zip(p, y_fix)]
+        if j + 1 < K:
+            x = less(x, entry, y)
+        store(vy, y, j, 0)
+        store(ys, y, j)
+        store(ps, [a + e for a, e in zip(p, load(av, j + 1))], j)
+        if j + 1 == K:
+            o_targets(j, send)
 
     ti = lax.broadcasted_iota(jnp.int32, (K, K), 0)
     tj = lax.broadcasted_iota(jnp.int32, (K, K), 1)
@@ -337,27 +350,33 @@
 
     for j in range(K):
         arrived(ob.at[j], o_recv.at[j])
+    o_ref[...] = ob[...]
+
+    @pl.when(c == 0)
+    def _():
+        panel_sends(sent)
+
+    for j in range(K):
+        for k in range(0 if j else 1, 2):
+            arrived(rnd.at[j, k, pl.ds(0, C - 1)], s_send.at[j, k])
+
+        @pl.loop(0, groups)
+        def _(g):
+            p_targets(j, g, sent)
+
+        o_targets(j, sent)
+
+
+def lay_out(o_ref, t_in, y_ref, v_ref, t_ref):
+    _, q, _, ng, G, _ = o_ref.shape
     for h in range(q):
         for n in range(ng):
             for s in range(G):
                 at = ((h * ng + n) * G + s) * LANES
                 for j in range(K):
-                    y_ref[j : j + 1, at : at + LANES] = ob[j, h, 0, n, s : s + 1, :]
-                    v_ref[j : j + 1, at : at + LANES] = ob[j, h, 1, n, s : s + 1, :]
-
-    @pl.when(c == 0)
-    def _():
-        panel_sends(sent)
-
-    for j in range(K):
-        for k in range(0 if j else 1, 2):
-            arrived(rnd.at[j, k, pl.ds(0, C - 1)], s_send.at[j, k])
-
-        @pl.loop(0, groups)
-        def _(g):
-            p_targets(j, g, sent)
-
-        o_targets(j, sent)
+                    y_ref[j : j + 1, at : at + LANES] = o_ref[j, h, 0, n, s : s + 1, :]
+                    v_ref[j : j + 1, at : at + LANES] = o_ref[j, h, 1, n, s : s + 1, :]
+    t_ref[...] = t_in[...]
 
 
 def solution(mesh):
@@ -369,15 +388,14 @@
         f32 = lambda *shape: pltpu.VMEM(shape, jnp.float32)
         dma = lambda *shape: pltpu.SemaphoreType.DMA(shape)
         nres = groups * (G - sp)
-        return pl.pallas_call(
+        blocks, t_block = pl.pallas_call(
             functools.partial(kernel, R, C),
             out_shape=(
-                jax.ShapeDtypeStruct((K, rows), jnp.float32),
-                jax.ShapeDtypeStruct((K, rows), jnp.float32),
+                jax.ShapeDtypeStruct((K, q, 2, ng, G, LANES), jnp.float32),
                 jax.ShapeDtypeStruct((K, K), jnp.float32),
             ),
             in_specs=[pl.BlockSpec(memory_space=pl.ANY)],
-            out_specs=(pl.BlockSpec(memory_space=pltpu.VMEM),) * 3,
+            out_specs=(pl.BlockSpec(memory_space=pltpu.VMEM),) * 2,
             scratch_shapes=[
                 f32(nres, LANES, cols),
                 f32(ring, LANES, cols),
@@ -410,6 +428,16 @@
                 collective_id=0, has_side_effects=True, vmem_limit_bytes=VMEM_BYTES
             ),
         )(matrix)
+        return pl.pallas_call(
+            lay_out,
+            out_shape=(
+                jax.ShapeDtypeStruct((K, rows), jnp.float32),
+                jax.ShapeDtypeStruct((K, rows), jnp.float32),
+                jax.ShapeDtypeStruct((K, K), jnp.float32),
+            ),
+            in_specs=[pl.BlockSpec(memory_space=pltpu.VMEM)] * 2,
+            out_specs=(pl.BlockSpec(memory_space=pltpu.VMEM),) * 3,
+        )(blocks, t_block)
 
     return jax.shard_map(
         on_device,

time: 76.5 us -> 73.3 us (0.958)
  local copies, waits for them, and re-layouts: 4.31 us -> 0 us
  Pallas kernels: 71.4 us -> 72.5 us
    unnamed x3 -> x0, local copies, waits for them, and re-layouts: 4.31 us -> none
    pallas_call x0 -> x1, Pallas kernels: none -> 1.74 us  [on_device(): pl.pallas_call(lay_out, out_shape=(jax.ShapeDtypeStruct((K, rows), jnp.fl...]
where the time goes in v2:
time: 73.3 us; the launch traced here: 73.1 us
  Pallas kernels  72.5 us (99%)
    pallas_call x1, Pallas kernels, on_device(): pl.pallas_call(functools.partial(kernel, R, C), out_shape=(jax.ShapeDtype...  70.7 us
    pallas_call x1, Pallas kernels, on_device(): pl.pallas_call(lay_out, out_shape=(jax.ShapeDtypeStruct((K, rows), jnp.fl...  1.74 us

profile of v2, /device:TPU:3, one launch (start us, length us, event | category | flops | bytes accessed | tf_op | source)
XLA Modules:
  0.0 73.1 jit_solution(4346351587690550575)
XLA Ops:
  0.6 70.7 %shard_map.38 = (f32[4,2,2,3,8,128]{5,4,3,2,1,0:T(8,128)}, f32[4,4]{1,0:T(4,128)}) custom-call(f32[6144,3072]{1,0:T(8,128)} %a_hbm.1), custom_call_target="tpu_custom_call" | custom-call | tf_op jit(solution)/shard_map/pallas_call | solution.py:391
  71.4 1.7 %shard_map.39 = (f32[4,6144]{1,0:T(4,128)}, f32[4,6144]{1,0:T(4,128)}, f32[4,4]{1,0:T(4,128)}) custom-call(f32[4,2,2,3,8,128]{5,4,3,2,1,0:T(8,128)} %get-tuple-element.5.o_ref, f32[4,4]{1,0:T(4,128)} %get-tuple-element.6.t_in), custom_call_target="tpu_custom_call" | custom-call | tf_op jit(solution)/shard_map/pallas_call | solution.py:431
